TPU v7x, 32 devices: a whole 2x2x4 slice. The times are simulated.
32 devices in a mesh: seg: 4 (over z), blk: 8 (over y, x, core).
Axes of the slice: x: 2, y: 2, z: 4, core: 2. Of those that a mesh axis runs over, the one named last changes fastest.
Arguments:
- train_acts: bfloat16 [4, 1024, 512], P('seg', 'blk'), may hold values from -6 to 6
- train_grads: bfloat16 [4, 1024, 4096], P('seg', 'blk'), may hold values from -0.0059814453 to 0.0059814453
- counts: int32 [8], replicated, may hold values from 1 to 2, as said below
- basis_in: bfloat16 [4, 1, 512, 512], P('seg'), may hold values from -1 to 1, as said below
- basis_out: bfloat16 [4, 8, 512, 512], P('seg', 'blk'), may hold values from -1 to 1, as said below
- eigenvalues: bfloat16 [4, 8, 512, 512], P('seg', 'blk'), may hold values from 0.049804688 to 5
- back_weight: bfloat16 [4, 8, 512, 512], P('seg', 'blk'), may hold values from -0.25 to 0.25
- derivative: bfloat16 [4, 4, 32, 4096], P('seg', None, None, 'blk'), may hold values from 0 to 1
- query_acts: bfloat16 [4, 4, 32, 512], P('seg'), may hold values from -6 to 6
- query_top: bfloat16 [4, 32, 4096], P(None, None, 'blk'), may hold values from -0.0059814453 to 0.0059814453
Outputs:
- scores: float32 [4, 16], P(None, 'blk')
Inputs may be any that keep to these rules, and one draw needn't show every extreme that they name: In each pair of indices 2k and 2k+1 of blk one count is 2 and the other 1, so all counts add up to 12; slots below a device's count are valid. `basis_in`: each 512 x 512 matrix is orthogonal up to rounding. `basis_out`: each 512 x 512 matrix is orthogonal up to rounding.
All inputs are finite; a program needn't handle non-finite values.
Results may differ from a plain program's by a relative error of at most 0.015.
Values may be sent and summed in bfloat16 or wider, within the bound.
A program may use at most 64 MiB of HBM per device.

v0:
```python
import math
import jax
import jax.numpy as jnp
from jax import lax
from jax.sharding import PartitionSpec as P

TB = 64
SLOTS = 2
damping = 0.05


def passed_along(value, axis, steps):
    count = lax.axis_size(axis)
    first, last = (max(0, -steps), min(count, count - steps))
    return lax.ppermute(value, axis, [(source, source + steps) for source in range(first, last)])


def advance(current, weight, derivs):
    queries, query_tok, blk_width = current.shape
    mixed = jnp.dot(
        current.reshape(queries * query_tok, blk_width), weight, preferred_element_type=jnp.float32
    )
    mixed = mixed.reshape(queries, query_tok, blk_width)
    return (current.astype(jnp.float32) + mixed * derivs.astype(jnp.float32)).astype(jnp.bfloat16)


def precondition(current, acts_seg, inner_basis, outer_basis, eigen_block):
    queries, query_tok, blk_width = current.shape
    in_slices = inner_basis.shape[0]
    in_width = in_slices * blk_width
    rot_err = jnp.dot(
        current.reshape(queries * query_tok, blk_width),
        outer_basis,
        preferred_element_type=jnp.float32,
    )
    rot_err = rot_err.astype(jnp.bfloat16).reshape(queries, query_tok, blk_width)
    act_split = acts_seg.reshape(queries, query_tok, in_slices, blk_width)
    rot_acts = jnp.einsum(
        "qtid,ide->qtie", act_split, inner_basis, preferred_element_type=jnp.float32
    ).astype(jnp.bfloat16)
    core_raw = jnp.einsum("qtd,qtie->qdie", rot_err, rot_acts, preferred_element_type=jnp.float32)
    core_raw = core_raw.reshape(queries, blk_width, in_width)
    scaled_core = (core_raw / (eigen_block.astype(jnp.float32)[None] + damping)).astype(
        jnp.bfloat16
    )
    left_prod = jnp.einsum(
        "cd,qdf->qcf", outer_basis, scaled_core, preferred_element_type=jnp.float32
    ).astype(jnp.bfloat16)
    left_split = left_prod.reshape(queries, blk_width, in_slices, blk_width)
    precond = jnp.einsum(
        "qcie,ife->qcif", left_split, inner_basis, preferred_element_type=jnp.float32
    )
    return precond.astype(jnp.bfloat16).reshape(queries, blk_width, in_width)


def block_scores(grad_rows, act_rows, precond, slot_tokens):
    row_count = grad_rows.shape[0]
    group_count = max(row_count // slot_tokens, 1)
    group_rows = row_count // group_count
    batch_groups = math.gcd(group_count, 8)
    grad_groups = grad_rows.reshape(
        group_count // batch_groups, batch_groups, group_rows, grad_rows.shape[1]
    )
    act_groups = act_rows.reshape(
        group_count // batch_groups, batch_groups, group_rows, act_rows.shape[1]
    )

    def one_batch(operands):
        grad_block, act_block = operands
        outer_prod = jnp.einsum(
            "btd,bte->bde", grad_block, act_block, preferred_element_type=jnp.float32
        ).astype(jnp.bfloat16)
        return jnp.einsum("bde,qde->bq", outer_prod, precond, preferred_element_type=jnp.float32)

    partial_scores = lax.map(one_batch, (grad_groups, act_groups))
    return (partial_scores.reshape(group_count, precond.shape[0]), group_rows)


def body(
    train_acts,
    train_grads,
    counts,
    basis_in,
    basis_out,
    eigenvalues,
    back_weight,
    derivative,
    query_acts,
    query_top,
):
    seg_count = lax.axis_size("seg")
    seg_index = lax.axis_index("seg")
    blk_index = lax.axis_index("blk")
    n_slot = lax.axis_size("blk") * SLOTS
    slot_ids = jnp.arange(n_slot, dtype=jnp.int32)
    current = query_top
    for relay_step in range(seg_count - 1):
        moved = advance(current, back_weight[0, 0], derivative[0])
        arrived = passed_along(moved, "seg", -1)
        current = jnp.where(seg_index == seg_count - 2 - relay_step, arrived, current)
    precond = precondition(current, query_acts[0], basis_in[0], basis_out[0, 0], eigenvalues[0, 0])
    exchanged = lax.all_to_all(train_grads, "blk", split_axis=2, concat_axis=1, tiled=True)
    grad_rows = exchanged[0]
    scores_part, group_rows = block_scores(
        grad_rows, lax.all_gather(train_acts, "blk", axis=1, tiled=True)[0], precond, TB
    )
    slot_of = jnp.arange(scores_part.shape[0], dtype=jnp.int32) * group_rows // TB
    placement = (slot_of[:, None] == slot_ids[None, :]).astype(jnp.float32)
    local_scores = jnp.dot(scores_part.T, placement, precision=lax.Precision.HIGHEST)
    mine = lax.psum_scatter(local_scores, "blk", scatter_dimension=1, tiled=True)
    mine = lax.psum(mine, "seg")
    own_valid = (jnp.arange(SLOTS, dtype=jnp.int32) < counts[blk_index]).astype(jnp.float32)
    return mine * own_valid[None, :]


def solution(mesh):
    in_specs = (
        P("seg", "blk", None),
        P("seg", "blk", None),
        P(),
        P("seg", None, None, None),
        P("seg", "blk", None, None),
        P("seg", "blk", None, None),
        P("seg", "blk", None, None),
        P("seg", None, None, "blk"),
        P("seg", None, None, None),
        P(None, None, "blk"),
    )
    out_specs = P(None, "blk")
    return jax.shard_map(body, mesh=mesh, in_specs=in_specs, out_specs=out_specs, check_vma=False)
```

profile of v0, /device:TPU:0, one launch (start us, length us, event | category | flops | bytes accessed | tf_op | source)
XLA Modules:
  0.0 125.0 jit_solution(6837176893961638313)
XLA Ops:
  6.5 1.4 %fusion.15 = bf16[4,32,512]{2,1,0:T(8,128)(2,1)S(1)} fusion(bf16[4,32,512]{2,1,0:T(8,128)(2,1)} %param.21, bf16[1,1,512,512]{3,2,1,0:T(8,128)(2,1)} %param.18, bf16[1,4,32,512]{3,2,1,0:T(8,128)(2,1)} %param.19), kind=kOutput, calls=%fused_computation.20 | convolution fusion | flops 67436544 | bytes 917504 | tf_op jit(solution)/shard_map/dot_general | solution.py:20
  8.0 1.3 %collective-permute-start = (bf16[4,32,512]{2,1,0:T(8,128)(2,1)S(1)}, bf16[4,32,512]{2,1,0:T(8,128)(2,1)S(1)}, u32[]{:S(2)}, u32[]{:S(2)}) collective-permute-start(bf16[4,32,512]{2,1,0:T(8,128)(2,1)S(1)} %fusion.15), channel_id=1, source_target_pairs={{8,0},{16,8},{24,16},{9,1},{17,9},{25,17},{10,2},{18,10},{26,18},{... | collective-permute-start | bytes 393224 | tf_op jit(solution)/shard_map/ppermute | solution.py:15
  9.3 5.0 %copy.25 = bf16[1,128,4096]{1,0,2:T(2,128)(2,1)S(1)} copy(bf16[1,128,4096]{2,1,0:T(8,128)(2,1)} %param.13) | data formatting | bytes 2097152 | tf_op args[1]
  14.8 23.4 %reduce = bf16[4096,128]{1,0:T(8,128)(2,1)} reduce(bf16[4096,1,128]{2,1,0:T(2,128)(2,1)S(1)} %bitcast.92, bf16[]{:T(256)} %broadcast.63), dimensions={1}, to_apply=%bitcast.73.reduce_sub_computation | reduce | bytes 2097154
  38.2 2.2 %reshape.95 = bf16[8,2,32768]{2,1,0:T(2,128)(2,1)} reshape(bf16[4096,128]{1,0:T(8,128)(2,1)} %reduce) | data formatting | bytes 2097152
  40.4 5.3 %all-to-all-start = ((bf16[8,2,32768]{2,1,0:T(2,128)(2,1)}), bf16[8,2,32768]{2,1,0:T(2,128)(2,1)}, u32[]{:S(2)}, u32[]{:S(2)}) async-start(bf16[8,2,32768]{2,1,0:T(2,128)(2,1)} %reshape.95), calls=%async_computation | async-start | bytes 2097152 | tf_op jit(solution)/shard_map/all_to_all | solution.py:102
  46.9 1.3 %collective-permute-start.1 = (bf16[4,32,512]{2,1,0:T(8,128)(2,1)S(1)}, bf16[4,32,512]{2,1,0:T(8,128)(2,1)S(1)}, u32[]{:S(2)}, u32[]{:S(2)}) collective-permute-start(bf16[4,32,512]{2,1,0:T(8,128)(2,1)S(1)} %add_convert_fusion.1), channel_id=1, source_target_pairs={{8,0},{16,8},{24,16},{9,1},{17,9},{25,17},{10,2},{18,10},{26,18},{... | collective-permute-start | bytes 393224 | tf_op jit(solution)/shard_map/ppermute | solution.py:15
  48.3 7.2 %collective-permute-done.1 = bf16[4,32,512]{2,1,0:T(8,128)(2,1)S(1)} collective-permute-done((bf16[4,32,512]{2,1,0:T(8,128)(2,1)S(1)}, bf16[4,32,512]{2,1,0:T(8,128)(2,1)S(1)}, u32[]{:S(2)}, u32[]{:S(2)}) %collective-permute-start.1) | collective-permute-done | bytes 131104 | tf_op jit(solution)/shard_map/ppermute | solution.py:15
  55.8 1.5 %collective-permute-start.2 = (bf16[4,32,512]{2,1,0:T(8,128)(2,1)S(1)}, bf16[4,32,512]{2,1,0:T(8,128)(2,1)S(1)}, u32[]{:S(2)}, u32[]{:S(2)}) collective-permute-start(bf16[4,32,512]{2,1,0:T(8,128)(2,1)S(1)} %add_convert_fusion), channel_id=1, source_target_pairs={{8,0},{16,8},{24,16},{9,1},{17,9},{25,17},{10,2},{18,10},{26,18},{... | collective-permute-start | bytes 393224 | tf_op jit(solution)/shard_map/ppermute | solution.py:15
  57.3 1.3 %fusion.16 = bf16[4,32,512]{2,1,0:T(8,128)(2,1)S(1)} fusion(bf16[1,1,512,512]{3,2,1,0:T(8,128)(2,1)} %param.15, bf16[1,4,32,512]{3,2,1,0:T(8,128)(2,1)S(1)} %copy-done.7), kind=kOutput, calls=%fused_computation.21 | convolution fusion | flops 67174400 | bytes 786432 | tf_op jit(solution)/shard_map/qtid,ide->qtie/dot_general | solution.py:38
  60.5 2.7 %collective-permute-done.2 = bf16[4,32,512]{2,1,0:T(8,128)(2,1)S(1)} collective-permute-done((bf16[4,32,512]{2,1,0:T(8,128)(2,1)S(1)}, bf16[4,32,512]{2,1,0:T(8,128)(2,1)S(1)}, u32[]{:S(2)}, u32[]{:S(2)}) %collective-permute-start.2) | collective-permute-done | bytes 131104 | tf_op jit(solution)/shard_map/ppermute | solution.py:15
  63.5 3.2 %fusion.13 = bf16[4,512,512]{2,1,0:T(8,128)(2,1)} fusion(bf16[4,32,512]{2,1,0:T(8,128)(2,1)S(1)} %bitcast.96, bf16[4,32,512]{2,1,0:T(8,128)(2,1)S(1)} %fusion.16, f32[512,512]{1,0:T(8,128)S(1)} %add_bitcast_fusion, bf16[1,1,512,512]{3,2,1,0:T(8,128)(2,1)S(1)} %copy-done), kind=kOutput, calls=%fused_computation.13 | convolution fusion | flops 1142947840 | bytes 3932160 | tf_op jit(solution)/shard_map/cd,qdf->qcf/dot_general | solution.py:46
  66.7 2.9 %fusion.10 = bf16[4,512,512]{2,1,0:T(8,128)(2,1)S(1)} fusion(bf16[4,512,512]{2,1,0:T(8,128)(2,1)} %fusion.13, bf16[1,1,512,512]{3,2,1,0:T(8,128)(2,1)S(1)} %copy-done.6), kind=kOutput, calls=%fused_computation.12 | convolution fusion | flops 1074790400 | bytes 4718592 | tf_op jit(solution)/shard_map/qcie,ife->qcif/dot_general | solution.py:50
  69.6 3.0 %copy.29 = bf16[4,512,512]{2,0,1:T(4,128)(2,1)} copy(bf16[4,512,512]{2,1,0:T(8,128)(2,1)S(1)} %fusion.10) | data formatting | bytes 4194304 | tf_op jit(solution)/shard_map/while | solution.py:75
  72.5 4.3 %reshape.96 = bf16[4096,1,128]{2,1,0:T(2,128)(2,1)S(1)} reshape(bf16[8,2,32768]{2,1,0:T(2,128)(2,1)} %all-to-all-done) | data formatting | bytes 2097152
  76.9 1.1 copy.35
  78.0 1.5 %copy.26 = bf16[1,8,128,512]{3,2,1,0:T(8,128)(2,1)S(1)} copy(bf16[1,8,128,512]{2,3,1,0:T(8,128)(2,1)} %bitcast.94) | data formatting | bytes 2097152 | tf_op jit(solution)/shard_map/all_to_all | solution.py:102
  79.5 12.8 %while.10 = (s32[]{:T(128)}, f32[2,8,4]{1,0,2:T(2,128)S(1)}, bf16[2,8,64,512]{3,2,1,0:T(8,128)(2,1)S(1)}, bf16[2,8,64,512]{3,2,1,0:T(8,128)(2,1)}, bf16[4,512,512]{2,0,1:T(4,128)(2,1)}, /*index=5*/s32[]{:T(128)}, s32[]{:T(128)}) while((s32[]{:T(128)}, f32[2,8,4]{1,0,2:T(2,128)S(1)}, bf16[2,8,64,512]{3,2,1,0:T(8,128)(2,1)S(1)}, ...), condition=%wide.region_1.2_spmd, body=%wide.region_0.1_spmd.sunk | while | flops 287309824 | bytes 19924460 | solution.py:75
  79.5 2.5 %convolution_convert_fusion.4 = bf16[8,512,512]{2,1,0:T(8,128)(2,1)S(1)} fusion(bf16[2,8,64,512]{3,2,1,0:T(8,128)(2,1)} %get-tuple-element.111, s32[]{:T(128)} %get-tuple-element.101, bf16[2,8,64,512]{3,2,1,0:T(8,128)(2,1)S(1)} %get-tuple-element.110), kind=kOutput, calls=%fused_computation.2.clone.1 | convolution fusion | flops 270532608 | bytes 5243904 | tf_op jit(solution)/shard_map/while/body/eval_jaxpr/btd,bte->bde/dot_general | solution.py:70
  82.0 3.8 %fusion.47 = f32[8,4,1]{0,1,2:T(4,128)S(1)} fusion(bf16[4,512,512]{2,0,1:T(4,128)(2,1)S(1)} %copy-done.2, bf16[8,512,512]{2,1,0:T(8,128)(2,1)S(1)} %convolution_convert_fusion.4), kind=kOutput, calls=%fused_computation.clone.1 | convolution fusion | flops 16777216 | bytes 6291584 | tf_op jit(solution)/shard_map/while/body/eval_jaxpr/bde,qde->bq/dot_general | solution.py:73
  85.9 2.5 %convolution_convert_fusion.4 = bf16[8,512,512]{2,1,0:T(8,128)(2,1)S(1)} fusion(bf16[2,8,64,512]{3,2,1,0:T(8,128)(2,1)} %get-tuple-element.111, s32[]{:T(128)} %get-tuple-element.101, bf16[2,8,64,512]{3,2,1,0:T(8,128)(2,1)S(1)} %get-tuple-element.110), kind=kOutput, calls=%fused_computation.2.clone.1 | convolution fusion | flops 270532608 | bytes 5243904 | tf_op jit(solution)/shard_map/while/body/eval_jaxpr/btd,bte->bde/dot_general | solution.py:70
  88.4 3.8 %fusion.47 = f32[8,4,1]{0,1,2:T(4,128)S(1)} fusion(bf16[4,512,512]{2,0,1:T(4,128)(2,1)S(1)} %copy-done.2, bf16[8,512,512]{2,1,0:T(8,128)(2,1)S(1)} %convolution_convert_fusion.4), kind=kOutput, calls=%fused_computation.clone.1 | convolution fusion | flops 16777216 | bytes 6291584 | tf_op jit(solution)/shard_map/while/body/eval_jaxpr/bde,qde->bq/dot_general | solution.py:73
  92.6 13.1 %all-reduce = f32[4,16]{0,1:T(8,128)S(1)} all-reduce(f32[4,16]{0,1:T(8,128)S(1)} %fusion.29), channel_id=2, replica_groups=mesh['seg'=4,'blk'=8] {'blk'}, use_global_device_ids=true, to_apply=%region_2.3.clone | all-reduce | flops 64 | bytes 512
  106.4 11.2 %psum.7 = f32[4,2]{0,1:T(2,128)S(1)} all-reduce(f32[4,2]{0,1:T(2,128)S(1)} %constant_dynamic-slice_fusion), channel_id=1, replica_groups=mesh['seg'=4,'blk'=8] {'seg'}, use_global_device_ids=true, to_apply=%region_3.4 | all-reduce | flops 8 | bytes 64 | tf_op jit(solution)/shard_map/psum | solution.py:111
  (45 shorter events, 5.2 us)
Async XLA Ops:
  6.5 56.7 %copy-start = (bf16[1,1,512,512]{3,2,1,0:T(8,128)(2,1)S(1)}, bf16[1,1,512,512]{3,2,1,0:T(8,128)(2,1)}, u32[]{:S(2)}) copy-start(bf16[1,1,512,512]{3,2,1,0:T(8,128)(2,1)} %param.16) | copy-start | bytes 1572868
  8.0 38.5 %collective-permute-start = (bf16[4,32,512]{2,1,0:T(8,128)(2,1)S(1)}, bf16[4,32,512]{2,1,0:T(8,128)(2,1)S(1)}, u32[]{:S(2)}, u32[]{:S(2)}) collective-permute-start(bf16[4,32,512]{2,1,0:T(8,128)(2,1)S(1)} %fusion.15), channel_id=1, source_target_pairs={{8,0},{16,8},{24,16},{9,1},{17,9},{25,17},{10,2},{18,10},{26,18},{... | collective-permute-start | bytes 393224 | tf_op jit(solution)/shard_map/ppermute | solution.py:15
  38.2 8.3 %copy-start.5 = (bf16[4,32,512]{2,1,0:T(8,128)(2,1)S(1)}, bf16[4,32,512]{2,1,0:T(8,128)(2,1)}, u32[]{:S(2)}) copy-start(bf16[4,32,512]{2,1,0:T(8,128)(2,1)} %param.21) | copy-start | bytes 393220
  38.2 8.4 %copy-start.1 = (bf16[1,1,512,512]{3,2,1,0:T(8,128)(2,1)S(1)}, bf16[1,1,512,512]{3,2,1,0:T(8,128)(2,1)}, u32[]{:S(2)}) copy-start(bf16[1,1,512,512]{3,2,1,0:T(8,128)(2,1)} %param.18) | copy-start | bytes 1572868
  38.2 8.4 %copy-start.4 = (bf16[1,4,32,512]{3,2,1,0:T(8,128)(2,1)S(1)}, bf16[1,4,32,512]{3,2,1,0:T(8,128)(2,1)}, u32[]{:S(2)}) copy-start(bf16[1,4,32,512]{3,2,1,0:T(8,128)(2,1)} %param.19) | copy-start | bytes 393220
  40.4 7.7 %copy-start.3 = (bf16[1,1,512,512]{3,2,1,0:T(8,128)(2,1)S(1)}, bf16[1,1,512,512]{3,2,1,0:T(8,128)(2,1)}, u32[]{:S(2)}) copy-start(bf16[1,1,512,512]{3,2,1,0:T(8,128)(2,1)} %param.17) | copy-start | bytes 1572868
  40.4 32.1 %all-to-all-start = ((bf16[8,2,32768]{2,1,0:T(2,128)(2,1)}), bf16[8,2,32768]{2,1,0:T(2,128)(2,1)}, u32[]{:S(2)}, u32[]{:S(2)}) async-start(bf16[8,2,32768]{2,1,0:T(2,128)(2,1)} %reshape.95), calls=%async_computation | async-start | bytes 2097152 | tf_op jit(solution)/shard_map/all_to_all | solution.py:102
  45.8 11.5 %copy-start.7 = (bf16[1,4,32,512]{3,2,1,0:T(8,128)(2,1)S(1)}, bf16[1,4,32,512]{3,2,1,0:T(8,128)(2,1)}, u32[]{:S(2)}) copy-start(bf16[1,4,32,512]{3,2,1,0:T(8,128)(2,1)} %param.20) | copy-start | bytes 393220
  45.8 33.7 %all-gather.2.cloned.1.call-start = ((), (), s32[]{:S(2)}) async-start(), calls=%async_computation.1 | async-start | bytes 1179648 | tf_op jit(solution)/shard_map/all_gather | solution.py:105
  46.6 12.0 %copy-start.9 = (u32[32]{0:T(128)S(1)}, u32[32]{0:T(128)}, u32[]{:S(2)}) copy-start(u32[32]{0:T(128)} %constant.56) | copy-start | bytes 388
  46.6 13.3 %copy-start.8 = (s32[8]{0:T(128)S(1)}, s32[8]{0:T(128)}, u32[]{:S(2)}) copy-start(s32[8]{0:T(128)} %param.14) | copy-start | bytes 100
  46.9 8.7 %collective-permute-start.1 = (bf16[4,32,512]{2,1,0:T(8,128)(2,1)S(1)}, bf16[4,32,512]{2,1,0:T(8,128)(2,1)S(1)}, u32[]{:S(2)}, u32[]{:S(2)}) collective-permute-start(bf16[4,32,512]{2,1,0:T(8,128)(2,1)S(1)} %add_convert_fusion.1), channel_id=1, source_target_pairs={{8,0},{16,8},{24,16},{9,1},{17,9},{25,17},{10,2},{18,10},{26,18},{... | collective-permute-start | bytes 393224 | tf_op jit(solution)/shard_map/ppermute | solution.py:15
  55.8 7.4 %collective-permute-start.2 = (bf16[4,32,512]{2,1,0:T(8,128)(2,1)S(1)}, bf16[4,32,512]{2,1,0:T(8,128)(2,1)S(1)}, u32[]{:S(2)}, u32[]{:S(2)}) collective-permute-start(bf16[4,32,512]{2,1,0:T(8,128)(2,1)S(1)} %add_convert_fusion), channel_id=1, source_target_pairs={{8,0},{16,8},{24,16},{9,1},{17,9},{25,17},{10,2},{18,10},{26,18},{... | collective-permute-start | bytes 393224 | tf_op jit(solution)/shard_map/ppermute | solution.py:15
  63.5 3.2 %copy-start.6 = (bf16[1,1,512,512]{3,2,1,0:T(8,128)(2,1)S(1)}, bf16[1,1,512,512]{3,2,1,0:T(8,128)(2,1)}, u32[]{:S(2)}) copy-start(bf16[1,1,512,512]{3,2,1,0:T(8,128)(2,1)} %param.15) | copy-start | bytes 1572868
  79.5 2.5 %copy-start.2 = (bf16[4,512,512]{2,0,1:T(4,128)(2,1)S(1)}, bf16[4,512,512]{2,0,1:T(4,128)(2,1)}, u32[]{:S(2)}) copy-start(bf16[4,512,512]{2,0,1:T(4,128)(2,1)} %get-tuple-element.112) | copy-start | bytes 6291460 | tf_op jit(solution)/shard_map/while
  85.9 2.5 %copy-start.2 = (bf16[4,512,512]{2,0,1:T(4,128)(2,1)S(1)}, bf16[4,512,512]{2,0,1:T(4,128)(2,1)}, u32[]{:S(2)}) copy-start(bf16[4,512,512]{2,0,1:T(4,128)(2,1)} %get-tuple-element.112) | copy-start | bytes 6291460 | tf_op jit(solution)/shard_map/while
Sparse Core Ops, SparseCore 0:
  48.5 26.8 all-gather.1
where the time goes:
time: 126 us; the launch traced here: 125 us
  other arithmetic  24.9 us (20%)
  blocking collectives  24.2 us (19%)
  matrix products  22.4 us (18%)
  local copies, waits for them, and re-layouts  19.1 us (15%)
  between operations  14.3 us (11%)
  waiting for transfers between devices  10.6 us (8%)
  starting transfers between devices  9.43 us (7%)
    unnamed x1, other arithmetic  23.4 us
    unnamed x25, local copies, waits for them, and re-layouts  13.9 us
    unnamed x1, blocking collectives  13.1 us
    psum x1, blocking collectives, body(): mine = lax.psum(mine, 'seg')  11.2 us
    ppermute x3, waiting for transfers between devices, passed_along(): lax.ppermute(value, axis, [(source, source + steps) for source in range(f...  9.91 us
    dot_general x2, matrix products, one_batch(): jnp.einsum('bde,qde->bq', outer_prod, precond, preferred_element_type=jnp...  7.62 us
    all_to_all x1, starting transfers between devices, body(): lax.all_to_all(train_grads, 'blk', split_axis=2, concat_axis=1, tiled=True)  5.33 us
    dot_general x2, matrix products, one_batch(): jnp.einsum('btd,bte->bde', grad_block, act_block, preferred_element_type=...  4.98 us
  transfers between devices with their start and end apart: 5, of which 2 were waited for; matrix products, arithmetic and copies ran while one was open for 40% of the time, Pallas kernels for 0%

commit v1 on v0

--- a/solution.py
+++ b/solution.py
@@ -7,6 +7,18 @@
 TB = 64
 SLOTS = 2
 damping = 0.05
+
+
+def in_blocks(x, dim, size):
+    shape = x.shape
+    blocks = x.reshape(*shape[:dim], size, shape[dim] // size, *shape[dim + 1 :])
+    return jnp.moveaxis(blocks, dim, 0)
+
+
+def joined_along(blocks, dim):
+    lengths = list(blocks.shape[1:])
+    lengths[dim] *= blocks.shape[0]
+    return jnp.moveaxis(blocks, 0, dim).reshape(lengths)
 
 
 def passed_along(value, axis, steps):
@@ -99,7 +111,16 @@
         arrived = passed_along(moved, "seg", -1)
         current = jnp.where(seg_index == seg_count - 2 - relay_step, arrived, current)
     precond = precondition(current, query_acts[0], basis_in[0], basis_out[0, 0], eigenvalues[0, 0])
-    exchanged = lax.all_to_all(train_grads, "blk", split_axis=2, concat_axis=1, tiled=True)
+    count_2, here = (lax.axis_size("blk"), lax.axis_index("blk"))
+    parts = in_blocks(train_grads, 2, count_2)
+    finished = [parts[here]]
+    for step in range(1, count_2):
+        sent = parts[(here + step) % count_2]
+        finished.append(
+            lax.ppermute(sent, "blk", [(i, (i + step) % count_2) for i in range(count_2)])
+        )
+    parts = jnp.stack(finished)[(here - jnp.arange(count_2)) % count_2]
+    exchanged = joined_along(parts, 1)
     grad_rows = exchanged[0]
     scores_part, group_rows = block_scores(
         grad_rows, lax.all_gather(train_acts, "blk", axis=1, tiled=True)[0], precond, TB

time: 126 us -> 105 us (0.83)
  other arithmetic: 24.9 us -> 2.48 us
  starting transfers between devices: 9.43 us -> 14 us
  local copies, waits for them, and re-layouts: 19.1 us -> 17.5 us
  matrix products: 22.4 us -> 23.9 us
    unnamed x1 -> x0, other arithmetic: 23.4 us -> none
    ppermute x0 -> x7, starting transfers between devices: none -> 9.85 us  [body(): lax.ppermute(sent, 'blk', [(i, (i + step) % count_2) for i in range(count...]
    unnamed x25 -> x26, local copies, waits for them, and re-layouts: 13.9 us -> 6.06 us
    another operation x0 -> x10, local copies, waits for them, and re-layouts: none -> 7.01 us
    all_to_all x1 -> x0, starting transfers between devices: 5.33 us -> none  [body(): lax.all_to_all(train_grads, 'blk', split_axis=2, concat_axis=1, tiled=True)]
    all_to_all x1 -> x0, local copies, waits for them, and re-layouts: 1.48 us -> none  [body(): lax.all_to_all(train_grads, 'blk', split_axis=2, concat_axis=1, tiled=True)]
    dot_general x1, matrix products: 3.21 us -> 4.56 us  [precondition(): jnp.einsum('cd,qdf->qcf', outer_basis, scaled_core, preferred_element_typ...]
  transfers between devices with their start and end apart: 5 -> 11, of which waited for: 2 -> 3; matrix products, arithmetic and copies ran while one was open for 40% -> 24% of each run, Pallas kernels for 0% -> 0%
where the time goes in v1:
time: 105 us
  matrix products  23.9 us (23%)
  blocking collectives  23 us (22%)
  local copies, waits for them, and re-layouts  17.5 us (17%)
  between operations  14.4 us (14%)
  starting transfers between devices  14 us (13%)
  waiting for transfers between devices  9.59 us (9%)
  other arithmetic  2.48 us (2%)
    unnamed x1, blocking collectives  12.1 us
    psum x1, blocking collectives, body(): mine = lax.psum(mine, 'seg')  10.8 us
    ppermute x7, starting transfers between devices, body(): lax.ppermute(sent, 'blk', [(i, (i + step) % count_2) for i in range(count...  9.85 us
    ppermute x3, waiting for transfers between devices, passed_along(): lax.ppermute(value, axis, [(source, source + steps) for source in range(f...  9.56 us
    dot_general x2, matrix products, one_batch(): jnp.einsum('bde,qde->bq', outer_prod, precond, preferred_element_type=jnp...  7.62 us
    another operation x9, local copies, waits for them, and re-layouts  7 us
    unnamed x26, local copies, waits for them, and re-layouts  6.06 us
    dot_general x2, matrix products, one_batch(): jnp.einsum('btd,bte->bde', grad_block, act_block, preferred_element_type=...  4.97 us
  transfers between devices with their start and end apart: 11, of which 3 were waited for; matrix products, arithmetic and copies ran while one was open for 24% of the time, Pallas kernels for 0%

profile of v1, /device:TPU:0, one launch (start us, length us, event | category | flops | bytes accessed | tf_op | source)
XLA Modules:
  0.0 104.9 jit_solution(17464067136881828164)
XLA Ops:
  6.5 1.7 %copy.30 = bf16[1,128,4096]{1,2,0:T(8,128)(2,1)S(1)} copy(bf16[1,128,4096]{2,1,0:T(8,128)(2,1)} %param.13) | data formatting | bytes 2097152 | tf_op args[1]
  9.1 1.7 %copy.32 = bf16[1,128,1,512]{3,1,2,0:T(8,128)(2,1)} copy(bf16[1,128,1,512]{1,3,2,0:T(8,128)(2,1)} %get-tuple-element.69) | data formatting | bytes 262144 | tf_op jit(solution)/shard_map/dynamic-slice.1
  11.3 1.7 %copy.33 = bf16[1,128,1,512]{3,1,2,0:T(8,128)(2,1)} copy(bf16[1,128,1,512]{1,3,2,0:T(8,128)(2,1)} %get-tuple-element.68) | data formatting | bytes 262144 | tf_op jit(solution)/shard_map/dynamic-slice.2
  12.9 2.5 %collective-permute-start.1 = (bf16[1,128,512]{2,1,0:T(8,128)(2,1)}, bf16[1,128,512]{2,1,0:T(8,128)(2,1)}, u32[]{:S(2)}, u32[]{:S(2)}) collective-permute-start(bf16[1,128,512]{2,1,0:T(8,128)(2,1)} %bitcast.8), channel_id=1, source_target_pairs={{0,2},{1,3},{2,4},{3,5},{4,6},{5,7},{6,0},{7,1},{8,10},{9,11},{10,... | collective-permute-start | bytes 393224 | tf_op jit(solution)/shard_map/ppermute | solution.py:120
  15.4 1.7 %copy.34 = bf16[1,128,1,512]{3,1,2,0:T(8,128)(2,1)} copy(bf16[1,128,1,512]{1,3,2,0:T(8,128)(2,1)} %get-tuple-element.67) | data formatting | bytes 262144 | tf_op jit(solution)/shard_map/dynamic-slice.3
  17.1 2.4 %collective-permute-start.2 = (bf16[1,128,512]{2,1,0:T(8,128)(2,1)}, bf16[1,128,512]{2,1,0:T(8,128)(2,1)}, u32[]{:S(2)}, u32[]{:S(2)}) collective-permute-start(bf16[1,128,512]{2,1,0:T(8,128)(2,1)} %bitcast.10), channel_id=1, source_target_pairs={{0,3},{1,4},{2,5},{3,6},{4,7},{5,0},{6,1},{7,2},{8,11},{9,12},{10,... | collective-permute-start | bytes 393224 | tf_op jit(solution)/shard_map/ppermute | solution.py:120
  21.7 1.4 %collective-permute-start.7 = (bf16[4,32,512]{2,1,0:T(8,128)(2,1)}, bf16[4,32,512]{2,1,0:T(8,128)(2,1)}, u32[]{:S(2)}, u32[]{:S(2)}) collective-permute-start(bf16[4,32,512]{2,1,0:T(8,128)(2,1)} %fusion.15), channel_id=1, source_target_pairs={{8,0},{16,8},{24,16},{9,1},{17,9},{25,17},{10,2},{18,10},{26,18},{... | collective-permute-start | bytes 393224 | tf_op jit(solution)/shard_map/ppermute | solution.py:27
  24.4 2.0 %fusion.16 = bf16[4,32,512]{2,1,0:T(8,128)(2,1)} fusion(bf16[1,1,512,512]{3,2,1,0:T(8,128)(2,1)} %param.15, bf16[1,4,32,512]{3,2,1,0:T(8,128)(2,1)} %param.20), kind=kOutput, calls=%fused_computation.22 | convolution fusion | flops 67174400 | bytes 786432 | tf_op jit(solution)/shard_map/qtid,ide->qtie/dot_general | solution.py:50
  29.3 1.6 %collective-permute-start.5 = (bf16[1,128,512]{2,1,0:T(8,128)(2,1)S(1)}, bf16[1,128,512]{2,1,0:T(8,128)(2,1)S(1)}, u32[]{:S(2)}, u32[]{:S(2)}) collective-permute-start(bf16[1,128,512]{2,1,0:T(8,128)(2,1)S(1)} %bitcast.118), channel_id=1, source_target_pairs={{0,6},{1,7},{2,0},{3,1},{4,2},{5,3},{6,4},{7,5},{8,14},{9,15},{10,... | collective-permute-start | bytes 393224 | tf_op jit(solution)/shard_map/ppermute | solution.py:120
  31.7 2.4 %collective-permute-start.6 = (bf16[1,128,512]{2,1,0:T(8,128)(2,1)S(1)}, bf16[1,128,512]{2,1,0:T(8,128)(2,1)S(1)}, u32[]{:S(2)}, u32[]{:S(2)}) collective-permute-start(bf16[1,128,512]{2,1,0:T(8,128)(2,1)S(1)} %bitcast.117), channel_id=1, source_target_pairs={{0,7},{1,0},{2,1},{3,2},{4,3},{5,4},{6,5},{7,6},{8,15},{9,8},{10,9... | collective-permute-start | bytes 393224 | tf_op jit(solution)/shard_map/ppermute | solution.py:120
  35.1 1.3 %collective-permute-start.8 = (bf16[4,32,512]{2,1,0:T(8,128)(2,1)S(1)}, bf16[4,32,512]{2,1,0:T(8,128)(2,1)S(1)}, u32[]{:S(2)}, u32[]{:S(2)}) collective-permute-start(bf16[4,32,512]{2,1,0:T(8,128)(2,1)S(1)} %add_convert_fusion.1), channel_id=1, source_target_pairs={{8,0},{16,8},{24,16},{9,1},{17,9},{25,17},{10,2},{18,10},{26,18},{... | collective-permute-start | bytes 393224 | tf_op jit(solution)/shard_map/ppermute | solution.py:27
  38.3 4.1 %collective-permute-done.8 = bf16[4,32,512]{2,1,0:T(8,128)(2,1)S(1)} collective-permute-done((bf16[4,32,512]{2,1,0:T(8,128)(2,1)S(1)}, bf16[4,32,512]{2,1,0:T(8,128)(2,1)S(1)}, u32[]{:S(2)}, u32[]{:S(2)}) %collective-permute-start.8) | collective-permute-done | bytes 131104 | tf_op jit(solution)/shard_map/ppermute | solution.py:27
  42.6 1.5 %collective-permute-start.9 = (bf16[4,32,512]{2,1,0:T(8,128)(2,1)S(1)}, bf16[4,32,512]{2,1,0:T(8,128)(2,1)S(1)}, u32[]{:S(2)}, u32[]{:S(2)}) collective-permute-start(bf16[4,32,512]{2,1,0:T(8,128)(2,1)S(1)} %add_convert_fusion), channel_id=1, source_target_pairs={{8,0},{16,8},{24,16},{9,1},{17,9},{25,17},{10,2},{18,10},{26,18},{... | collective-permute-start | bytes 393224 | tf_op jit(solution)/shard_map/ppermute | solution.py:27
  44.8 5.2 %collective-permute-done.9 = bf16[4,32,512]{2,1,0:T(8,128)(2,1)S(1)} collective-permute-done((bf16[4,32,512]{2,1,0:T(8,128)(2,1)S(1)}, bf16[4,32,512]{2,1,0:T(8,128)(2,1)S(1)}, u32[]{:S(2)}, u32[]{:S(2)}) %collective-permute-start.9) | collective-permute-done | bytes 131104 | tf_op jit(solution)/shard_map/ppermute | solution.py:27
  50.3 4.6 %fusion.13 = bf16[4,512,512]{2,1,0:T(8,128)(2,1)} fusion(bf16[4,32,512]{2,1,0:T(8,128)(2,1)S(1)} %bitcast.120, bf16[4,32,512]{2,1,0:T(8,128)(2,1)} %fusion.16, f32[512,512]{1,0:T(8,128)} %add_bitcast_fusion, bf16[1,1,512,512]{3,2,1,0:T(8,128)(2,1)S(1)} %copy-done), kind=kOutput, calls=%fused_computation.14 | convolution fusion | flops 1142947840 | bytes 3932160 | tf_op jit(solution)/shard_map/cd,qdf->qcf/dot_general | solution.py:58
  54.8 2.9 %fusion.10 = bf16[4,512,512]{2,1,0:T(8,128)(2,1)S(1)} fusion(bf16[4,512,512]{2,1,0:T(8,128)(2,1)} %fusion.13, bf16[1,1,512,512]{3,2,1,0:T(8,128)(2,1)S(1)} %copy-done.6), kind=kOutput, calls=%fused_computation.13 | convolution fusion | flops 1074790400 | bytes 4718592 | tf_op jit(solution)/shard_map/qcie,ife->qcif/dot_general | solution.py:62
  57.7 3.0 %copy.41 = bf16[4,512,512]{2,0,1:T(4,128)(2,1)} copy(bf16[4,512,512]{2,1,0:T(8,128)(2,1)S(1)} %fusion.10) | data formatting | bytes 4194304 | tf_op jit(solution)/shard_map/while | solution.py:87
  60.7 12.7 %while.10 = (s32[]{:T(128)}, f32[2,8,4]{1,0,2:T(2,128)S(1)}, bf16[2,8,64,512]{3,2,1,0:T(8,128)(2,1)S(1)}, bf16[2,8,64,512]{3,2,1,0:T(8,128)(2,1)}, bf16[4,512,512]{2,0,1:T(4,128)(2,1)}, /*index=5*/s32[]{:T(128)}, s32[]{:T(128)}) while((s32[]{:T(128)}, f32[2,8,4]{1,0,2:T(2,128)S(1)}, bf16[2,8,64,512]{3,2,1,0:T(8,128)(2,1)S(1)}, ...), condition=%wide.region_1.2_spmd, body=%wide.region_0.1_spmd.sunk | while | flops 287309824 | bytes 19924460 | solution.py:87
  60.7 2.5 %convolution_convert_fusion.4 = bf16[8,512,512]{2,1,0:T(8,128)(2,1)S(1)} fusion(bf16[2,8,64,512]{3,2,1,0:T(8,128)(2,1)} %get-tuple-element.119, s32[]{:T(128)} %get-tuple-element.109, bf16[2,8,64,512]{3,2,1,0:T(8,128)(2,1)S(1)} %get-tuple-element.118), kind=kOutput, calls=%fused_computation.3.clone.1 | convolution fusion | flops 270532608 | bytes 5243904 | tf_op jit(solution)/shard_map/while/body/eval_jaxpr/btd,bte->bde/dot_general | solution.py:82
  63.2 3.8 %fusion.49 = f32[8,4,1]{0,1,2:T(4,128)S(1)} fusion(bf16[4,512,512]{2,0,1:T(4,128)(2,1)S(1)} %copy-done.2, bf16[8,512,512]{2,1,0:T(8,128)(2,1)S(1)} %convolution_convert_fusion.4), kind=kOutput, calls=%fused_computation.1.clone.1 | convolution fusion | flops 16777216 | bytes 6291584 | tf_op jit(solution)/shard_map/while/body/eval_jaxpr/bde,qde->bq/dot_general | solution.py:85
  67.1 2.5 %convolution_convert_fusion.4 = bf16[8,512,512]{2,1,0:T(8,128)(2,1)S(1)} fusion(bf16[2,8,64,512]{3,2,1,0:T(8,128)(2,1)} %get-tuple-element.119, s32[]{:T(128)} %get-tuple-element.109, bf16[2,8,64,512]{3,2,1,0:T(8,128)(2,1)S(1)} %get-tuple-element.118), kind=kOutput, calls=%fused_computation.3.clone.1 | convolution fusion | flops 270532608 | bytes 5243904 | tf_op jit(solution)/shard_map/while/body/eval_jaxpr/btd,bte->bde/dot_general | solution.py:82
  69.6 3.8 %fusion.49 = f32[8,4,1]{0,1,2:T(4,128)S(1)} fusion(bf16[4,512,512]{2,0,1:T(4,128)(2,1)S(1)} %copy-done.2, bf16[8,512,512]{2,1,0:T(8,128)(2,1)S(1)} %convolution_convert_fusion.4), kind=kOutput, calls=%fused_computation.1.clone.1 | convolution fusion | flops 16777216 | bytes 6291584 | tf_op jit(solution)/shard_map/while/body/eval_jaxpr/bde,qde->bq/dot_general | solution.py:85
  73.8 12.1 %all-reduce = f32[4,16]{0,1:T(8,128)S(1)} all-reduce(f32[4,16]{0,1:T(8,128)S(1)} %fusion.29), channel_id=2, replica_groups=mesh['seg'=4,'blk'=8] {'blk'}, use_global_device_ids=true, to_apply=%region_2.3.clone | all-reduce | flops 64 | bytes 512
  86.6 10.8 %psum.7 = f32[4,2]{0,1:T(2,128)S(1)} all-reduce(f32[4,2]{0,1:T(2,128)S(1)} %constant_dynamic-slice_fusion.8), channel_id=1, replica_groups=mesh['seg'=4,'blk'=8] {'seg'}, use_global_device_ids=true, to_apply=%region_3.4 | all-reduce | flops 8 | bytes 64 | tf_op jit(solution)/shard_map/psum | solution.py:132
  (69 shorter events, 13.5 us)
Async XLA Ops:
  6.5 43.5 %copy-start = (bf16[1,1,512,512]{3,2,1,0:T(8,128)(2,1)S(1)}, bf16[1,1,512,512]{3,2,1,0:T(8,128)(2,1)}, u32[]{:S(2)}) copy-start(bf16[1,1,512,512]{3,2,1,0:T(8,128)(2,1)} %param.16) | copy-start | bytes 1572868
  6.5 54.1 %all-gather.2.cloned.1.call-start = ((), (), s32[]{:S(2)}) async-start(), calls=%async_computation | async-start | bytes 1179648 | tf_op jit(solution)/shard_map/all_gather | solution.py:126
  8.2 12.5 %copy-start.1 = (bf16[1,1,512,512]{3,2,1,0:T(8,128)(2,1)S(1)}, bf16[1,1,512,512]{3,2,1,0:T(8,128)(2,1)}, u32[]{:S(2)}) copy-start(bf16[1,1,512,512]{3,2,1,0:T(8,128)(2,1)} %param.18) | copy-start | bytes 1572868
  8.2 12.5 %copy-start.4 = (bf16[1,4,32,512]{3,2,1,0:T(8,128)(2,1)S(1)}, bf16[1,4,32,512]{3,2,1,0:T(8,128)(2,1)}, u32[]{:S(2)}) copy-start(bf16[1,4,32,512]{3,2,1,0:T(8,128)(2,1)} %param.19) | copy-start | bytes 393220
  8.2 12.5 %copy-start.5 = (bf16[4,32,512]{2,1,0:T(8,128)(2,1)S(1)}, bf16[4,32,512]{2,1,0:T(8,128)(2,1)}, u32[]{:S(2)}) copy-start(bf16[4,32,512]{2,1,0:T(8,128)(2,1)} %param.21) | copy-start | bytes 393220
  8.3 15.0 %copy-start.3 = (bf16[1,1,512,512]{3,2,1,0:T(8,128)(2,1)S(1)}, bf16[1,1,512,512]{3,2,1,0:T(8,128)(2,1)}, u32[]{:S(2)}) copy-start(bf16[1,1,512,512]{3,2,1,0:T(8,128)(2,1)} %param.17) | copy-start | bytes 1572868
  10.8 18.5 %collective-permute-start = (bf16[1,128,512]{2,1,0:T(8,128)(2,1)}, bf16[1,128,512]{2,1,0:T(8,128)(2,1)}, u32[]{:S(2)}, u32[]{:S(2)}) collective-permute-start(bf16[1,128,512]{2,1,0:T(8,128)(2,1)} %bitcast.6), channel_id=1, source_target_pairs={{0,1},{1,2},{2,3},{3,4},{4,5},{5,6},{6,7},{7,0},{8,9},{9,10},{10,1... | collective-permute-start | bytes 393224 | tf_op jit(solution)/shard_map/ppermute | solution.py:120
  12.9 18.8 %collective-permute-start.1 = (bf16[1,128,512]{2,1,0:T(8,128)(2,1)}, bf16[1,128,512]{2,1,0:T(8,128)(2,1)}, u32[]{:S(2)}, u32[]{:S(2)}) collective-permute-start(bf16[1,128,512]{2,1,0:T(8,128)(2,1)} %bitcast.8), channel_id=1, source_target_pairs={{0,2},{1,3},{2,4},{3,5},{4,6},{5,7},{6,0},{7,1},{8,10},{9,11},{10,... | collective-permute-start | bytes 393224 | tf_op jit(solution)/shard_map/ppermute | solution.py:120
  17.1 18.0 %collective-permute-start.2 = (bf16[1,128,512]{2,1,0:T(8,128)(2,1)}, bf16[1,128,512]{2,1,0:T(8,128)(2,1)}, u32[]{:S(2)}, u32[]{:S(2)}) collective-permute-start(bf16[1,128,512]{2,1,0:T(8,128)(2,1)} %bitcast.10), channel_id=1, source_target_pairs={{0,3},{1,4},{2,5},{3,6},{4,7},{5,0},{6,1},{7,2},{8,11},{9,12},{10,... | collective-permute-start | bytes 393224 | tf_op jit(solution)/shard_map/ppermute | solution.py:120
  20.2 17.0 %collective-permute-start.3 = (bf16[1,128,512]{2,1,0:T(8,128)(2,1)}, bf16[1,128,512]{2,1,0:T(8,128)(2,1)}, u32[]{:S(2)}, u32[]{:S(2)}) collective-permute-start(bf16[1,128,512]{2,1,0:T(8,128)(2,1)} %bitcast.12), channel_id=1, source_target_pairs={{0,4},{1,5},{2,6},{3,7},{4,0},{5,1},{6,2},{7,3},{8,12},{9,13},{10,... | collective-permute-start | bytes 393224 | tf_op jit(solution)/shard_map/ppermute | solution.py:120
  21.7 5.1 %copy-start.7 = (s32[8]{0:T(128)S(1)}, s32[8]{0:T(128)}, u32[]{:S(2)}) copy-start(s32[8]{0:T(128)} %param.14) | copy-start | bytes 100
  21.7 5.8 %copy-start.8 = (u32[32]{0:T(128)S(1)}, u32[32]{0:T(128)}, u32[]{:S(2)}) copy-start(u32[32]{0:T(128)} %constant.108) | copy-start | bytes 388
  21.7 7.3 %collective-permute-start.7 = (bf16[4,32,512]{2,1,0:T(8,128)(2,1)}, bf16[4,32,512]{2,1,0:T(8,128)(2,1)}, u32[]{:S(2)}, u32[]{:S(2)}) collective-permute-start(bf16[4,32,512]{2,1,0:T(8,128)(2,1)} %fusion.15), channel_id=1, source_target_pairs={{8,0},{16,8},{24,16},{9,1},{17,9},{25,17},{10,2},{18,10},{26,18},{... | collective-permute-start | bytes 393224 | tf_op jit(solution)/shard_map/ppermute | solution.py:27
  29.0 9.2 %collective-permute-start.4 = (bf16[1,128,512]{2,1,0:T(8,128)(2,1)S(1)}, bf16[1,128,512]{2,1,0:T(8,128)(2,1)S(1)}, u32[]{:S(2)}, u32[]{:S(2)}) collective-permute-start(bf16[1,128,512]{2,1,0:T(8,128)(2,1)S(1)} %bitcast.119), channel_id=1, source_target_pairs={{0,5},{1,6},{2,7},{3,0},{4,1},{5,2},{6,3},{7,4},{8,13},{9,14},{10,... | collective-permute-start | bytes 393224 | tf_op jit(solution)/shard_map/ppermute | solution.py:120
  29.3 9.0 %collective-permute-start.5 = (bf16[1,128,512]{2,1,0:T(8,128)(2,1)S(1)}, bf16[1,128,512]{2,1,0:T(8,128)(2,1)S(1)}, u32[]{:S(2)}, u32[]{:S(2)}) collective-permute-start(bf16[1,128,512]{2,1,0:T(8,128)(2,1)S(1)} %bitcast.118), channel_id=1, source_target_pairs={{0,6},{1,7},{2,0},{3,1},{4,2},{5,3},{6,4},{7,5},{8,14},{9,15},{10,... | collective-permute-start | bytes 393224 | tf_op jit(solution)/shard_map/ppermute | solution.py:120
  31.7 12.4 %collective-permute-start.6 = (bf16[1,128,512]{2,1,0:T(8,128)(2,1)S(1)}, bf16[1,128,512]{2,1,0:T(8,128)(2,1)S(1)}, u32[]{:S(2)}, u32[]{:S(2)}) collective-permute-start(bf16[1,128,512]{2,1,0:T(8,128)(2,1)S(1)} %bitcast.117), channel_id=1, source_target_pairs={{0,7},{1,0},{2,1},{3,2},{4,3},{5,4},{6,5},{7,6},{8,15},{9,8},{10,9... | collective-permute-start | bytes 393224 | tf_op jit(solution)/shard_map/ppermute | solution.py:120
  35.1 7.3 %collective-permute-start.8 = (bf16[4,32,512]{2,1,0:T(8,128)(2,1)S(1)}, bf16[4,32,512]{2,1,0:T(8,128)(2,1)S(1)}, u32[]{:S(2)}, u32[]{:S(2)}) collective-permute-start(bf16[4,32,512]{2,1,0:T(8,128)(2,1)S(1)} %add_convert_fusion.1), channel_id=1, source_target_pairs={{8,0},{16,8},{24,16},{9,1},{17,9},{25,17},{10,2},{18,10},{26,18},{... | collective-permute-start | bytes 393224 | tf_op jit(solution)/shard_map/ppermute | solution.py:27
  42.6 7.3 %collective-permute-start.9 = (bf16[4,32,512]{2,1,0:T(8,128)(2,1)S(1)}, bf16[4,32,512]{2,1,0:T(8,128)(2,1)S(1)}, u32[]{:S(2)}, u32[]{:S(2)}) collective-permute-start(bf16[4,32,512]{2,1,0:T(8,128)(2,1)S(1)} %add_convert_fusion), channel_id=1, source_target_pairs={{8,0},{16,8},{24,16},{9,1},{17,9},{25,17},{10,2},{18,10},{26,18},{... | collective-permute-start | bytes 393224 | tf_op jit(solution)/shard_map/ppermute | solution.py:27
  50.2 4.6 %copy-start.6 = (bf16[1,1,512,512]{3,2,1,0:T(8,128)(2,1)S(1)}, bf16[1,1,512,512]{3,2,1,0:T(8,128)(2,1)}, u32[]{:S(2)}) copy-start(bf16[1,1,512,512]{3,2,1,0:T(8,128)(2,1)} %param.15) | copy-start | bytes 1572868
  60.7 2.5 %copy-start.2 = (bf16[4,512,512]{2,0,1:T(4,128)(2,1)S(1)}, bf16[4,512,512]{2,0,1:T(4,128)(2,1)}, u32[]{:S(2)}) copy-start(bf16[4,512,512]{2,0,1:T(4,128)(2,1)} %get-tuple-element.120) | copy-start | bytes 6291460 | tf_op jit(solution)/shard_map/while
  67.1 2.5 %copy-start.2 = (bf16[4,512,512]{2,0,1:T(4,128)(2,1)S(1)}, bf16[4,512,512]{2,0,1:T(4,128)(2,1)}, u32[]{:S(2)}) copy-start(bf16[4,512,512]{2,0,1:T(4,128)(2,1)} %get-tuple-element.120) | copy-start | bytes 6291460 | tf_op jit(solution)/shard_map/while
Sparse Core Ops, SparseCore 0:
  23.2 30.8 all-gather.1
